TPU v7x, 32 devices: a whole 2x2x4 slice. The times are simulated.
32 devices in a mesh: dp: 4 (over x, core), seq: 4 (over z), chan: 2 (over y).
Axes of the slice: x: 2, y: 2, z: 4, core: 2. Of those that a mesh axis runs over, the one named last changes fastest.
Arguments:
- inputs: bfloat16 [4, 8, 256, 2048], P('dp', 'seq', None, 'chan'), may hold values from -6 to 6
- cotangent: bfloat16 [4, 8, 256, 2048], P('dp', 'seq', None, 'chan'), may hold values from -6 to 6
- rows_in: bfloat16 [256, 256], replicated, may hold values from -0.375 to 0.375
- cols_mix: bfloat16 [8, 8], replicated, may hold values from -2 to 2
- blocks_gate: bfloat16 [4, 512, 512], P('chan'), may hold values from -0.25 to 0.25
- blocks_up: bfloat16 [4, 512, 512], P('chan'), may hold values from -0.25 to 0.25
- mix_gate: bfloat16 [4, 4, 512], replicated, may hold values from -3 to 3
- mix_up: bfloat16 [4, 4, 512], replicated, may hold values from -3 to 3
Outputs:
- input_grad: bfloat16 [4, 8, 256, 2048], P('dp', 'seq', None, 'chan')
- rows_grad: float32 [256, 256], replicated
- cols_grad: float32 [8, 8], replicated
- blocks_gate_grad: float32 [4, 512, 512], P('chan')
- blocks_up_grad: float32 [4, 512, 512], P('chan')
- mix_gate_grad: float32 [4, 4, 512], P(None, 'chan')
- mix_up_grad: float32 [4, 4, 512], P(None, 'chan')
All inputs are finite; a program needn't handle non-finite values.
Results may differ from a plain program's by a relative error of at most 0.011.
Values may be sent and summed in bfloat16 or wider, within the bound.
No kernel may reach another device: no remote copies, remote signals or barrier semaphores. Data moves between devices by JAX's collectives and lax.ppermute only.
A program may use at most 128 MiB of HBM per device.

v0:
```python
import math
import jax
import jax.numpy as jnp
from jax import lax
from jax.sharding import PartitionSpec as P


def column_keep(segment, cols_mix):
    mixed = jnp.einsum(
        "er,brcd->becd", cols_mix, segment, preferred_element_type=jnp.float32
    ).astype(jnp.bfloat16)
    return (segment, mixed)


def body(inputs, cotangent, rows_in, cols_mix, blocks_gate, blocks_up, mix_gate, mix_up):
    batch_dev, rows_dev, cols_all, width_dev = inputs.shape
    block_size = blocks_gate.shape[1]
    local_blocks = blocks_gate.shape[0]
    chan_index = lax.axis_index("chan")
    split_shape = (batch_dev, rows_dev, cols_all, local_blocks, block_size)
    first = jnp.einsum("ec,brcd->bred", rows_in, inputs, preferred_element_type=jnp.float32).astype(
        jnp.bfloat16
    )
    first_cols, second_cols = column_keep(
        lax.all_to_all(first, "seq", split_axis=2, concat_axis=1, tiled=True), cols_mix
    )
    second_rows = lax.all_to_all(second_cols, "seq", split_axis=1, concat_axis=2, tiled=True)
    hidden = (inputs.astype(jnp.float32) + second_rows.astype(jnp.float32)).astype(jnp.bfloat16)
    hidden_blocks = hidden.reshape(split_shape)
    gate_rows_own = lax.dynamic_slice_in_dim(
        mix_gate, chan_index * local_blocks, local_blocks, 0
    ).astype(jnp.float32)
    up_rows_own = lax.dynamic_slice_in_dim(
        mix_up, chan_index * local_blocks, local_blocks, 0
    ).astype(jnp.float32)
    gate_mid = jnp.einsum(
        "brckj,kjl->brckl", hidden_blocks, blocks_gate, preferred_element_type=jnp.float32
    ).astype(jnp.bfloat16)
    up_mid = jnp.einsum(
        "brckj,kjl->brckl", hidden_blocks, blocks_up, preferred_element_type=jnp.float32
    ).astype(jnp.bfloat16)
    gate_add = jnp.einsum(
        "mkj,brckj->brcmj",
        gate_rows_own,
        lax.all_gather(gate_mid, "chan", axis=3, tiled=True).astype(jnp.float32),
    )
    up_add = jnp.einsum(
        "mkj,brckj->brcmj",
        up_rows_own,
        lax.all_gather(up_mid, "chan", axis=3, tiled=True).astype(jnp.float32),
    )
    upstream = cotangent.astype(jnp.float32).reshape(split_shape)
    sigma = jax.nn.sigmoid(gate_add)
    up_grad = (upstream * gate_add * sigma).astype(jnp.bfloat16)
    gate_grad = (upstream * up_add * sigma * (1.0 + gate_add * (1.0 - sigma))).astype(jnp.bfloat16)
    gate_all, up_all = (
        lax.all_gather(gate_grad, "chan", axis=3, tiled=True),
        lax.all_gather(up_grad, "chan", axis=3, tiled=True),
    )
    gate_cols_own = lax.dynamic_slice_in_dim(
        mix_gate, chan_index * local_blocks, local_blocks, 1
    ).astype(jnp.float32)
    up_cols_own = lax.dynamic_slice_in_dim(
        mix_up, chan_index * local_blocks, local_blocks, 1
    ).astype(jnp.float32)
    mix_gate_sum = jnp.einsum(
        "brcmj,brckj->mkj", gate_all, gate_mid, preferred_element_type=jnp.float32
    )
    mix_up_sum = jnp.einsum("brcmj,brckj->mkj", up_all, up_mid, preferred_element_type=jnp.float32)
    gate_back = jnp.einsum("mkj,brcmj->brckj", gate_cols_own, gate_all.astype(jnp.float32)).astype(
        jnp.bfloat16
    )
    up_back = jnp.einsum("mkj,brcmj->brckj", up_cols_own, up_all.astype(jnp.float32)).astype(
        jnp.bfloat16
    )
    blocks_gate_sum = jnp.einsum(
        "brckj,brckl->kjl", hidden_blocks, gate_back, preferred_element_type=jnp.float32
    )
    blocks_up_sum = jnp.einsum(
        "brckj,brckl->kjl", hidden_blocks, up_back, preferred_element_type=jnp.float32
    )
    hidden_grad = (
        upstream
        + jnp.einsum("brckl,kjl->brckj", gate_back, blocks_gate, preferred_element_type=jnp.float32)
        + jnp.einsum("brckl,kjl->brckj", up_back, blocks_up, preferred_element_type=jnp.float32)
    )
    hidden_grad = hidden_grad.reshape(inputs.shape).astype(jnp.bfloat16)
    segment = lax.all_to_all(hidden_grad, "seq", split_axis=2, concat_axis=1, tiled=True)
    mixed = jnp.einsum(
        "er,becd->brcd", cols_mix, segment, preferred_element_type=jnp.float32
    ).astype(jnp.bfloat16)
    cols_sum = jnp.einsum("becd,brcd->er", segment, first_cols, preferred_element_type=jnp.float32)
    first_grad = lax.all_to_all(mixed, "seq", split_axis=1, concat_axis=2, tiled=True)
    rows_sum = jnp.einsum("bred,brcd->ec", first_grad, inputs, preferred_element_type=jnp.float32)
    input_grad = (
        hidden_grad.astype(jnp.float32)
        + jnp.einsum("ec,bred->brcd", rows_in, first_grad, preferred_element_type=jnp.float32)
    ).astype(jnp.bfloat16)
    rows_total, cols_total = lax.psum((rows_sum, cols_sum), ("dp", "seq", "chan"))
    gate_blocks_total, up_blocks_total, gate_mix_total, up_mix_total = lax.psum(
        (blocks_gate_sum, blocks_up_sum, mix_gate_sum, mix_up_sum), ("dp", "seq")
    )
    count_dp = lax.axis_size("dp")
    count_seq = lax.axis_size("seq")
    count_chan = lax.axis_size("chan")
    batch_all = batch_dev * count_dp
    rows_all = rows_dev * count_seq
    width_all = width_dev * count_chan
    rows_scale = 1.0 / math.sqrt(batch_all * rows_all * width_all)
    cols_scale = 1.0 / math.sqrt(batch_all * cols_all * width_all)
    block_scale = 1.0 / math.sqrt(batch_all * rows_all * cols_all)
    return (
        input_grad,
        rows_total * rows_scale,
        cols_total * cols_scale,
        gate_blocks_total * block_scale,
        up_blocks_total * block_scale,
        gate_mix_total * block_scale,
        up_mix_total * block_scale,
    )


def solution(mesh):
    in_specs = (
        P("dp", "seq", None, "chan"),
        P("dp", "seq", None, "chan"),
        P(),
        P(),
        P("chan", None, None),
        P("chan", None, None),
        P(),
        P(),
    )
    out_specs = (
        P("dp", "seq", None, "chan"),
        P(),
        P(),
        P("chan", None, None),
        P("chan", None, None),
        P(None, "chan", None),
        P(None, "chan", None),
    )
    return jax.shard_map(body, mesh=mesh, in_specs=in_specs, out_specs=out_specs, check_vma=False)
```

profile of v0, /device:TPU:0, one launch (start us, length us, event | category | flops | bytes accessed | tf_op | source)
XLA Modules:
  0.0 618.1 jit_solution(10451862501799467449)
XLA Ops:
  7.2 1.8 fusion.36
  10.1 31.8 %all_to_all.54 = bf16[1,2,256,1024]{3,1,0,2:T(2,128)(2,1)S(1)} all-to-all(bf16[1,2,256,1024]{3,1,0,2:T(2,128)(2,1)S(1)} %copy.163), channel_id=1, replica_groups=mesh['dp'=4,'seq'=4,'chan'=2] {'seq'}, dimensions={2} | all-to-all | bytes 2097152 | tf_op jit(solution)/shard_map/all_to_all | solution.py:25
  44.9 27.8 %all_to_all.55 = bf16[1,8,64,1024]{3,2,0,1:T(8,128)(2,1)S(1)} all-to-all(bf16[1,8,64,1024]{3,2,0,1:T(8,128)(2,1)S(1)} %copy.166), channel_id=1, replica_groups=mesh['dp'=4,'seq'=4,'chan'=2] {'seq'}, dimensions={1} | all-to-all | bytes 2097152 | tf_op jit(solution)/shard_map/all_to_all | solution.py:27
  75.5 2.7 reshape.142
  78.2 2.4 copy.197
  80.7 1.8 convolution_convert_fusion.2
  82.5 1.7 convolution_convert_fusion.1
  87.2 1.6 copy.173
  88.8 26.0 %all-gather.5.cloned.1.call-done = bf16[1,2,256,4,512]{4,2,1,0,3:T(8,128)(2,1)} async-done(((bf16[1,2,256,2,512]{4,2,1,0,3:T(8,128)(2,1)}), bf16[1,2,256,4,512]{4,2,1,0,3:T(8,128)(2,1)}) %all-gather.5.cloned.1.call-update) | async-done | bytes 2097168 | tf_op jit(solution)/shard_map/all_gather | solution.py:50
  114.8 4.5 copy.170
  119.3 4.2 fusion.14
  123.5 4.2 copy.172
  127.7 22.4 %all-gather.7.cloned.1.call-done = bf16[1,2,256,4,512]{4,2,1,0,3:T(8,128)(2,1)} async-done(((bf16[1,2,256,2,512]{4,2,1,0,3:T(8,128)(2,1)}), bf16[1,2,256,4,512]{4,2,1,0,3:T(8,128)(2,1)}) %all-gather.7.cloned.1.call-update) | async-done | bytes 2097168 | tf_op jit(solution)/shard_map/all_gather | solution.py:45
  150.1 4.5 copy.176
  154.6 4.1 fusion.12
  158.7 4.1 copy.178
  162.9 5.0 fusion.10
  169.0 2.3 copy.179
  171.3 1.6 copy.183
  173.4 28.8 %all-gather.11.cloned.1.call-done = bf16[1,2,256,4,512]{4,2,1,0,3:T(8,128)(2,1)} async-done(((bf16[1,2,256,2,512]{4,2,1,0,3:T(8,128)(2,1)}), bf16[1,2,256,4,512]{4,2,1,0,3:T(8,128)(2,1)}) %all-gather.11.cloned.1.call-update) | async-done | bytes 2097168 | tf_op jit(solution)/shard_map/all_gather | solution.py:58
  202.2 4.5 copy.186
  206.7 3.9 fusion.30
  210.5 2.5 copy.188
  213.1 24.3 %all-gather.9.cloned.1.call-done = bf16[1,2,256,4,512]{4,2,1,0,3:T(8,128)(2,1)} async-done(((bf16[1,2,256,2,512]{4,2,1,0,3:T(8,128)(2,1)}), bf16[1,2,256,4,512]{4,2,1,0,3:T(8,128)(2,1)}) %all-gather.9.cloned.1.call-update) | async-done | bytes 2097168 | tf_op jit(solution)/shard_map/all_gather | solution.py:57
  237.3 4.5 copy.180
  241.8 3.8 fusion.33
  245.6 3.7 copy.182
  249.3 2.1 fusion.45
  252.8 2.2 copy.190
  254.9 4.6 all-to-all-start.2
  259.6 2.0 convolution_bitcast_fusion
  261.6 2.0 convolution_bitcast_fusion.1
  264.9 2.1 copy.201
  267.0 2.1 copy.202
  269.1 23.6 %all-to-all-done.2 = bf16[1,2,256,1024]{3,1,0,2:T(2,128)(2,1)} async-done(((bf16[1,2,256,1024]{3,1,0,2:T(2,128)(2,1)}), bf16[1,2,256,1024]{3,1,0,2:T(2,128)(2,1)}, u32[]{:S(2)}, u32[]{:S(2)}) %all-to-all-start.2) | async-done | bytes 1048608 | tf_op jit(solution)/shard_map/all_to_all | solution.py:88
  296.3 1.5 copy.194
  297.8 4.3 all-to-all-start.3
  302.1 5.5 fusion.39
  307.6 3.5 fusion.42
  311.1 120.2 %all-reduce = (f32[4,2,512]{0,1,2:T(2,128)}, f32[4,2,512]{0,1,2:T(2,128)}) all-reduce(f32[4,2,512]{0,1,2:T(2,128)} %fusion.39, f32[4,2,512]{0,1,2:T(2,128)} %fusion.42), channel_id=1, replica_groups=mesh['dp'=4,'seq'=4,'chan'=2] {'dp','seq'}, use_global_device_ids=true, to_apply=%region_4.0 | all-reduce | flops 8192 | bytes 65536 | tf_op jit(solution)/shard_map/psum | solution.py:100
  431.3 2.7 broadcast_multiply_fusion.2
  434.0 1.8 copy.204
  435.9 1.8 copy.205
  438.5 36.9 %psum.43 = f32[8,8]{1,0:T(8,128)S(1)} all-reduce(f32[8,8]{1,0:T(8,128)S(1)} %convolution_bitcast_fusion.3), channel_id=1, replica_groups=mesh['dp'=4,'seq'=4,'chan'=2] {'dp','seq','chan'}, use_global_device_ids=true, to_apply=%region_1.0 | all-reduce | flops 64 | bytes 512 | tf_op jit(solution)/shard_map/psum | solution.py:99
  475.9 4.7 broadcast_multiply_fusion
  484.9 2.3 copy.203
  487.2 122.4 %all-reduce.5.cloned.1.call-done = f32[256,256]{1,0:T(8,128)} async-done(((f32[256,256]{1,0:T(8,128)}), f32[256,256]{1,0:T(8,128)}) %all-reduce.5.cloned.1.call-update) | async-done | bytes 262160 | tf_op jit(solution)/shard_map/psum | solution.py:99
  609.6 1.7 broadcast_multiply_fusion.4
  (84 shorter events, 23.0 us)
Async XLA Ops:
  7.2 75.4 %copy-start = (bf16[2,512,512]{2,1,0:T(8,128)(2,1)S(1)}, bf16[2,512,512]{2,1,0:T(8,128)(2,1)}, u32[]{:S(2)}) copy-start(bf16[2,512,512]{2,1,0:T(8,128)(2,1)} %param.12) | copy-start | bytes 3145732
  7.2 107.7 %all-gather.5.cloned.1.call-start = ((), (), s32[]{:S(2)}) async-start(), calls=%async_computation.4 | async-start | bytes 3145728 | tf_op jit(solution)/shard_map/all_gather | solution.py:50
  42.3 1.6 copy-start.19
  43.8 1.0 copy-start.2
  72.9 1.2 copy-start.8
  75.5 5.1 copy-start.12
  82.4 2.1 copy-start.17
  82.5 3.0 copy-start.18
  82.5 67.6 %all-gather.7.cloned.1.call-start = ((), (), s32[]{:S(2)}) async-start(), calls=%async_computation.5 | async-start | bytes 3145728 | tf_op jit(solution)/shard_map/all_gather | solution.py:45
  84.3 117.9 %all-gather.11.cloned.1.call-start = ((), (), s32[]{:S(2)}) async-start(), calls=%async_computation.7 | async-start | bytes 3145728 | tf_op jit(solution)/shard_map/all_gather | solution.py:58
  168.9 68.4 %all-gather.9.cloned.1.call-start = ((), (), s32[]{:S(2)}) async-start(), calls=%async_computation.6 | async-start | bytes 3145728 | tf_op jit(solution)/shard_map/all_gather | solution.py:57
  213.0 38.4 %copy-start.6 = (bf16[2,256,2,512]{3,1,0,2:T(8,128)(2,1)}, bf16[2,256,2,512]{3,1,0,2:T(8,128)(2,1)S(1)}, u32[]{:S(2)}) copy-start(bf16[2,256,2,512]{3,1,0,2:T(8,128)(2,1)S(1)} %copy.188) | copy-start | bytes 3145732
  249.3 2.1 copy-start.11
  249.3 2.2 copy-start.13
  252.8 6.8 %copy-start.7 = (bf16[2,256,2,512]{3,1,0,2:T(8,128)(2,1)S(1)}, bf16[2,256,2,512]{3,1,0,2:T(8,128)(2,1)}, u32[]{:S(2)}) copy-start(bf16[2,256,2,512]{3,1,0,2:T(8,128)(2,1)} %copy-done.6) | copy-start | bytes 3145732
  254.9 37.7 %all-to-all-start.2 = ((bf16[1,2,256,1024]{3,1,0,2:T(2,128)(2,1)}), bf16[1,2,256,1024]{3,1,0,2:T(2,128)(2,1)}, u32[]{:S(2)}, u32[]{:S(2)}) async-start(bf16[1,2,256,1024]{3,1,0,2:T(2,128)(2,1)} %copy.190), calls=%async_computation.2 | async-start | bytes 2097152 | tf_op jit(solution)/shard_map/all_to_all | solution.py:88
  259.5 216.4 %all-reduce.7.cloned.1.call-start = ((), (), s32[]{:S(2)}) async-start(), calls=%async_computation.9 | async-start | bytes 8388608 | tf_op jit(solution)/shard_map/psum | solution.py:100
  259.6 2.0 copy-start.10
  263.6 1.2 copy-start.5
  263.7 3.3 copy-start.4
  297.8 182.9 %all-to-all-start.3 = ((bf16[1,8,64,1024]{3,2,0,1:T(8,128)(2,1)}), bf16[1,8,64,1024]{3,2,0,1:T(8,128)(2,1)}, u32[]{:S(2)}, u32[]{:S(2)}) async-start(bf16[1,8,64,1024]{3,2,0,1:T(8,128)(2,1)} %copy.194), calls=%async_computation.3 | async-start | bytes 2097152 | tf_op jit(solution)/shard_map/all_to_all | solution.py:93
  302.1 5.5 copy-start.15
  302.1 307.5 %all-reduce.5.cloned.1.call-start = ((), (), s32[]{:S(2)}) async-start(), calls=%async_computation.8 | async-start | bytes 524288 | tf_op jit(solution)/shard_map/psum | solution.py:99
  302.1 5.5 copy-start.14
  311.1 126.6 %copy-start.3 = (bf16[8,64,1024]{2,0,1:T(8,128)(2,1)S(1)}, bf16[8,64,1024]{2,0,1:T(8,128)(2,1)}, u32[]{:S(2)}) copy-start(bf16[8,64,1024]{2,0,1:T(8,128)(2,1)} %copy-done.2) | copy-start | bytes 3145732
  480.7 1.5 copy-start.9
  480.7 2.7 copy-start.16
  483.4 127.9 %copy-start.1 = (bf16[2,512,512]{2,1,0:T(8,128)(2,1)S(1)}, bf16[2,512,512]{2,1,0:T(8,128)(2,1)}, u32[]{:S(2)}) copy-start(bf16[2,512,512]{2,1,0:T(8,128)(2,1)} %param.12) | copy-start | bytes 3145732
Sparse Core Ops, SparseCore 0:
  82.6 32.2 all-gather.4
  117.0 33.1 all-gather.6
  169.0 33.1 all-gather.10
  204.2 33.1 all-gather.8
  264.4 161.0 all-reduce.6
  483.5 126.0 all-reduce.4
where the time goes:
time: 620 us; the launch traced here: 618 us
  waiting for transfers between devices  248 us (40%)
  blocking collectives  217 us (35%)
  local copies, waits for them, and re-layouts  72.1 us (12%)
  matrix products  41.5 us (7%)
  other arithmetic  16.3 us (3%)
  between operations  14.5 us (2%)
  starting transfers between devices  9.24 us (1%)
    psum x1, waiting for transfers between devices, body(): lax.psum((rows_sum, cols_sum), ('dp', 'seq', 'chan'))  122 us
    psum x1, blocking collectives, body(): lax.psum((blocks_gate_sum, blocks_up_sum, mix_gate_sum, mix_up_sum), ('dp...  120 us
    psum x1, blocking collectives, body(): lax.psum((rows_sum, cols_sum), ('dp', 'seq', 'chan'))  36.9 us
    all_to_all x1, blocking collectives, body(): lax.all_to_all(first, 'seq', split_axis=2, concat_axis=1, tiled=True)  31.8 us
    all_gather x1, waiting for transfers between devices, body(): lax.all_gather(up_grad, 'chan', axis=3, tiled=True)  28.8 us
    all_to_all x1, blocking collectives, body(): lax.all_to_all(second_cols, 'seq', split_axis=1, concat_axis=2, tiled=True)  27.8 us
    all_gather x1, waiting for transfers between devices, body(): lax.all_gather(up_mid, 'chan', axis=3, tiled=True).astype(jnp.float32)  26 us
    all_gather x1, waiting for transfers between devices, body(): lax.all_gather(gate_grad, 'chan', axis=3, tiled=True)  24.3 us
  transfers between devices with their start and end apart: 8, of which 6 were waited for; matrix products, arithmetic and copies ran while one was open for 12% of the time, Pallas kernels for 0%

commit v1 on v0

--- a/solution.py
+++ b/solution.py
@@ -3,6 +3,29 @@
 import jax.numpy as jnp
 from jax import lax
 from jax.sharding import PartitionSpec as P
+
+
+def in_order(blocks, dim):
+    dims = list(blocks.shape[1:])
+    dims[dim] *= blocks.shape[0]
+    return jnp.moveaxis(blocks, 0, dim).reshape(dims)
+
+
+def collected_by_bits(x, axis):
+    length, index = (lax.axis_size(axis), lax.axis_index(axis))
+    blocks, distance = (x[None], 1)
+    while distance < length:
+        partner_block = lax.ppermute(blocks, axis, [(i, i ^ distance) for i in range(length)])
+        low = index & distance == 0
+        blocks = jnp.concatenate(
+            [jnp.where(low, blocks, partner_block), jnp.where(low, partner_block, blocks)]
+        )
+        distance *= 2
+    return blocks
+
+
+def doubled_up(shard, axis, dim):
+    return in_order(collected_by_bits(shard, axis), dim)
 
 
 def column_keep(segment, cols_mix):
@@ -54,7 +77,7 @@
     up_grad = (upstream * gate_add * sigma).astype(jnp.bfloat16)
     gate_grad = (upstream * up_add * sigma * (1.0 + gate_add * (1.0 - sigma))).astype(jnp.bfloat16)
     gate_all, up_all = (
-        lax.all_gather(gate_grad, "chan", axis=3, tiled=True),
+        doubled_up(gate_grad, "chan", 3),
         lax.all_gather(up_grad, "chan", axis=3, tiled=True),
     )
     gate_cols_own = lax.dynamic_slice_in_dim(

time: 620 us -> 603 us (0.973)
  waiting for transfers between devices: 248 us -> 225 us
    ppermute x0 -> x1, waiting for transfers between devices: none -> 34.8 us  [collected_by_bits(): lax.ppermute(blocks, axis, [(i, i ^ distance) for i in range(length)])]
    all_gather x1, waiting for transfers between devices: 28.8 us -> 0.01 us  [body(): lax.all_gather(up_grad, 'chan', axis=3, tiled=True)]
    all_gather x1 -> x0, waiting for transfers between devices: 24.3 us -> none  [body(): lax.all_gather(gate_grad, 'chan', axis=3, tiled=True)]
    another operation x8 -> x9, local copies, waits for them, and re-layouts: 16.4 us -> 19.7 us
  transfers between devices with their start and end apart: 8 -> 8, of which waited for: 6 -> 5; matrix products, arithmetic and copies ran while one was open for 12% -> 13% of each run, Pallas kernels for 0% -> 0%
where the time goes in v1:
time: 603 us; the launch traced here: 602 us
  waiting for transfers between devices  225 us (37%)
  blocking collectives  217 us (36%)
  local copies, waits for them, and re-layouts  71.5 us (12%)
  matrix products  45.8 us (8%)
  other arithmetic  18.3 us (3%)
  between operations  14.2 us (2%)
  starting transfers between devices  9.35 us (2%)
    psum x1, waiting for transfers between devices, body(): lax.psum((rows_sum, cols_sum), ('dp', 'seq', 'chan'))  123 us
    psum x1, blocking collectives, body(): lax.psum((blocks_gate_sum, blocks_up_sum, mix_gate_sum, mix_up_sum), ('dp...  119 us
    psum x1, blocking collectives, body(): lax.psum((rows_sum, cols_sum), ('dp', 'seq', 'chan'))  38.2 us
    ppermute x1, waiting for transfers between devices, collected_by_bits(): lax.ppermute(blocks, axis, [(i, i ^ distance) for i in range(length)])  34.8 us
    all_to_all x1, blocking collectives, body(): lax.all_to_all(first, 'seq', split_axis=2, concat_axis=1, tiled=True)  31.8 us
    all_to_all x1, blocking collectives, body(): lax.all_to_all(second_cols, 'seq', split_axis=1, concat_axis=2, tiled=True)  27.8 us
    all_gather x1, waiting for transfers between devices, body(): lax.all_gather(up_mid, 'chan', axis=3, tiled=True).astype(jnp.float32)  26 us
    all_gather x1, waiting for transfers between devices, body(): lax.all_gather(gate_mid, 'chan', axis=3, tiled=True).astype(jnp.float32)  22.3 us
  transfers between devices with their start and end apart: 8, of which 5 were waited for; matrix products, arithmetic and copies ran while one was open for 13% of the time, Pallas kernels for 0%

profile of v1, /device:TPU:0, one launch (start us, length us, event | category | flops | bytes accessed | tf_op | source)
XLA Modules:
  0.0 601.7 jit_solution(6779276690325321726)
XLA Ops:
  7.2 1.8 fusion.27
  10.1 31.8 %all_to_all.54 = bf16[1,2,256,1024]{3,1,0,2:T(2,128)(2,1)S(1)} all-to-all(bf16[1,2,256,1024]{3,1,0,2:T(2,128)(2,1)S(1)} %copy.168), channel_id=1, replica_groups=mesh['dp'=4,'seq'=4,'chan'=2] {'seq'}, dimensions={2} | all-to-all | bytes 2097152 | tf_op jit(solution)/shard_map/all_to_all | solution.py:48
  44.9 27.8 %all_to_all.55 = bf16[1,8,64,1024]{3,2,0,1:T(8,128)(2,1)S(1)} all-to-all(bf16[1,8,64,1024]{3,2,0,1:T(8,128)(2,1)S(1)} %copy.171), channel_id=1, replica_groups=mesh['dp'=4,'seq'=4,'chan'=2] {'seq'}, dimensions={1} | all-to-all | bytes 2097152 | tf_op jit(solution)/shard_map/all_to_all | solution.py:50
  75.5 2.7 reshape.145
  78.2 2.4 copy.202
  80.7 1.8 convolution_convert_fusion.3
  82.5 1.7 convolution_convert_fusion.2
  85.5 1.7 copy.166
  87.2 1.6 copy.178
  88.8 26.0 %all-gather.4.cloned.1.call-done = bf16[1,2,256,4,512]{4,2,1,0,3:T(8,128)(2,1)} async-done(((bf16[1,2,256,2,512]{4,2,1,0,3:T(8,128)(2,1)}), bf16[1,2,256,4,512]{4,2,1,0,3:T(8,128)(2,1)}) %all-gather.4.cloned.1.call-update) | async-done | bytes 2097168 | tf_op jit(solution)/shard_map/all_gather | solution.py:73
  114.8 4.5 copy.175
  119.3 4.2 fusion.14
  123.5 4.3 copy.177
  127.8 22.3 %all-gather.6.cloned.1.call-done = bf16[1,2,256,4,512]{4,2,1,0,3:T(8,128)(2,1)} async-done(((bf16[1,2,256,2,512]{4,2,1,0,3:T(8,128)(2,1)}), bf16[1,2,256,4,512]{4,2,1,0,3:T(8,128)(2,1)}) %all-gather.6.cloned.1.call-update) | async-done | bytes 2097168 | tf_op jit(solution)/shard_map/all_gather | solution.py:68
  150.1 4.5 copy.181
  154.6 4.1 fusion.12
  158.7 4.1 copy.183
  162.9 5.0 fusion.10
  169.2 1.6 copy.188
  171.3 34.8 %collective-permute-done = bf16[1,1,2,256,2,512]{5,3,4,2,1,0:T(8,128)(2,1)} collective-permute-done((bf16[1,1,2,256,2,512]{5,3,4,2,1,0:T(8,128)(2,1)}, bf16[1,1,2,256,2,512]{5,3,4,2,1,0:T(8,128)(2,1)}, u32[]{:S(2)}, u32[]{:S(2)}) %collective-permute-start) | collective-permute-done | bytes 1048608 | tf_op jit(solution)/shard_map/ppermute | solution.py:18
  206.1 1.7 broadcast_select_fusion.1
  209.6 4.5 copy.186
  214.1 3.8 fusion.23
  217.9 2.4 copy.187
  220.3 2.1 fusion.33
  222.4 4.6 copy.191
  227.0 3.8 fusion.24
  230.8 2.5 copy.193
  233.3 3.9 fusion.1
  238.8 2.2 copy.195
  240.9 4.6 all-to-all-start.2
  245.5 3.3 convolution_bitcast_fusion.1
  248.8 2.0 convolution_bitcast_fusion
  252.0 2.1 copy.206
  254.1 2.1 copy.208
  256.2 19.0 %all-to-all-done.2 = bf16[1,2,256,1024]{3,1,0,2:T(2,128)(2,1)} async-done(((bf16[1,2,256,1024]{3,1,0,2:T(2,128)(2,1)}), bf16[1,2,256,1024]{3,1,0,2:T(2,128)(2,1)}, u32[]{:S(2)}, u32[]{:S(2)}) %all-to-all-start.2) | async-done | bytes 1048608 | tf_op jit(solution)/shard_map/all_to_all | solution.py:111
  280.4 4.3 all-to-all-start.3
  284.7 5.4 convolution_bitcast_fusion.2
  290.1 3.5 fusion.30
  293.7 119.4 %all-reduce = (f32[4,2,512]{0,1,2:T(2,128)}, f32[4,2,512]{0,1,2:T(2,128)}) all-reduce(f32[4,2,512]{0,1,2:T(2,128)} %convolution_bitcast_fusion.2, f32[4,2,512]{0,1,2:T(2,128)} %fusion.30), channel_id=1, replica_groups=mesh['dp'=4,'seq'=4,'chan'=2] {'dp','seq'}, use_global_device_ids=true, to_apply=%region_4.5 | all-reduce | flops 8192 | bytes 65536 | tf_op jit(solution)/shard_map/psum | solution.py:123
  413.1 2.8 broadcast_multiply_fusion.2
  415.8 1.8 copy.210
  417.6 1.8 copy.211
  420.2 38.2 %psum.43 = f32[8,8]{1,0:T(8,128)S(1)} all-reduce(f32[8,8]{1,0:T(8,128)S(1)} %convolution_bitcast_fusion.4), channel_id=1, replica_groups=mesh['dp'=4,'seq'=4,'chan'=2] {'dp','seq','chan'}, use_global_device_ids=true, to_apply=%region_1.2 | all-reduce | flops 64 | bytes 512 | tf_op jit(solution)/shard_map/psum | solution.py:122
  459.1 4.7 broadcast_multiply_fusion
  468.0 2.3 copy.209
  470.3 123.2 %all-reduce.5.cloned.1.call-done = f32[256,256]{1,0:T(8,128)} async-done(((f32[256,256]{1,0:T(8,128)}), f32[256,256]{1,0:T(8,128)}) %all-reduce.5.cloned.1.call-update) | async-done | bytes 262160 | tf_op jit(solution)/shard_map/psum | solution.py:122
  593.5 1.7 broadcast_multiply_fusion.4
  (79 shorter events, 25.0 us)
Async XLA Ops:
  7.2 75.4 %copy-start = (bf16[2,512,512]{2,1,0:T(8,128)(2,1)S(1)}, bf16[2,512,512]{2,1,0:T(8,128)(2,1)}, u32[]{:S(2)}) copy-start(bf16[2,512,512]{2,1,0:T(8,128)(2,1)} %param.12) | copy-start | bytes 3145732
  7.2 107.7 %all-gather.4.cloned.1.call-start = ((), (), s32[]{:S(2)}) async-start(), calls=%async_computation.4 | async-start | bytes 3145728 | tf_op jit(solution)/shard_map/all_gather | solution.py:73
  42.3 1.6 copy-start.16
  43.8 1.0 copy-start.2
  72.9 1.2 copy-start.6
  75.5 5.1 copy-start.9
  82.5 1.9 copy-start.15
  82.5 2.8 copy-start.14
  82.5 67.6 %all-gather.6.cloned.1.call-start = ((), (), s32[]{:S(2)}) async-start(), calls=%async_computation.5 | async-start | bytes 3145728 | tf_op jit(solution)/shard_map/all_gather | solution.py:68
  84.3 138.1 %all-gather.8.cloned.1.call-start = ((), (), s32[]{:S(2)}) async-start(), calls=%async_computation.6 | async-start | bytes 3145728 | tf_op jit(solution)/shard_map/all_gather | solution.py:81
  167.9 38.3 %collective-permute-start = (bf16[1,1,2,256,2,512]{5,3,4,2,1,0:T(8,128)(2,1)}, bf16[1,1,2,256,2,512]{5,3,4,2,1,0:T(8,128)(2,1)}, u32[]{:S(2)}, u32[]{:S(2)}) collective-permute-start(bf16[1,1,2,256,2,512]{5,3,4,2,1,0:T(8,128)(2,1)} %get-tuple-element.47), channel_id=1, source_target_pairs={{0,1},{1,0},{2,3},{3,2},{4,5},{5,4},{6,7},{7,6},{8,9},{9,8},{10,11... | collective-permute-start | bytes 3145736 | tf_op jit(solution)/shard_map/ppermute | solution.py:18
  220.3 2.1 copy-start.8
  230.8 2.5 copy-start.10
  240.9 34.4 %all-to-all-start.2 = ((bf16[1,2,256,1024]{3,1,0,2:T(2,128)(2,1)}), bf16[1,2,256,1024]{3,1,0,2:T(2,128)(2,1)}, u32[]{:S(2)}, u32[]{:S(2)}) async-start(bf16[1,2,256,1024]{3,1,0,2:T(2,128)(2,1)} %copy.195), calls=%async_computation.2 | async-start | bytes 2097152 | tf_op jit(solution)/shard_map/all_to_all | solution.py:111
  245.5 213.5 %all-reduce.7.cloned.1.call-start = ((), (), s32[]{:S(2)}) async-start(), calls=%async_computation.8 | async-start | bytes 8388608 | tf_op jit(solution)/shard_map/psum | solution.py:123
  250.8 1.2 copy-start.5
  250.8 3.3 copy-start.4
  280.4 183.4 %all-to-all-start.3 = ((bf16[1,8,64,1024]{3,2,0,1:T(8,128)(2,1)}), bf16[1,8,64,1024]{3,2,0,1:T(8,128)(2,1)}, u32[]{:S(2)}, u32[]{:S(2)}) async-start(bf16[1,8,64,1024]{3,2,0,1:T(8,128)(2,1)} %copy.199), calls=%async_computation.3 | async-start | bytes 2097152 | tf_op jit(solution)/shard_map/all_to_all | solution.py:116
  284.6 5.5 copy-start.12
  284.7 308.9 %all-reduce.5.cloned.1.call-start = ((), (), s32[]{:S(2)}) async-start(), calls=%async_computation.7 | async-start | bytes 524288 | tf_op jit(solution)/shard_map/psum | solution.py:122
  284.7 5.4 copy-start.11
  293.7 125.8 %copy-start.3 = (bf16[8,64,1024]{2,0,1:T(8,128)(2,1)S(1)}, bf16[8,64,1024]{2,0,1:T(8,128)(2,1)}, u32[]{:S(2)}) copy-start(bf16[8,64,1024]{2,0,1:T(8,128)(2,1)} %copy-done.2) | copy-start | bytes 3145732
  463.8 1.5 copy-start.7
  463.8 2.7 copy-start.13
  466.5 128.6 %copy-start.1 = (bf16[2,512,512]{2,1,0:T(8,128)(2,1)S(1)}, bf16[2,512,512]{2,1,0:T(8,128)(2,1)}, u32[]{:S(2)}) copy-start(bf16[2,512,512]{2,1,0:T(8,128)(2,1)} %param.12) | copy-start | bytes 3145732
Sparse Core Ops, SparseCore 0:
  82.6 32.2 all-gather.3
  117.0 33.1 all-gather.5
  169.4 46.2 all-gather.7
  250.9 159.1 all-reduce.6
  466.7 126.8 all-reduce.4
